TPU v7x, 256 devices: a whole 4x4x8 slice. The times are simulated.
256 devices in a mesh: energy: 32 (over z_hi, x, y), cell: 8 (over z_lo, core).
Axes of the slice: x: 4, y: 4, z: 8 (z_hi: 2, z_lo: 4; z = z_hi * 4 + z_lo), core: 2. Of those that a mesh axis runs over, the one named last changes fastest.
Arguments:
- green_pair: float32 [4, 32, 16, 256, 256], P(None, 'energy', 'cell'), may hold values from -4 to 4
- retarded_diag: float32 [2, 32, 16, 256, 256], P(None, 'energy', 'cell'), may hold values from -0.25 to 0.25
- retarded_upper: float32 [2, 32, 16, 256, 256], P(None, 'energy', 'cell'), may hold values from -0.25 to 0.25
- coulomb_diag: float32 [16, 256, 256], P('cell'), may hold values from -0.375 to 0.375
- coulomb_upper: float32 [16, 256, 256], P('cell'), may hold values from -0.375 to 0.375
Outputs:
- lesser_new: float32 [2, 32, 16, 256, 256], P(None, 'energy', 'cell')
All inputs are finite; a program needn't handle non-finite values.
Results may differ from a plain program's by a relative error of at most 0.00014.
Values sent between devices are 32-bit elements; how exact they have to be, the bound alone decides.
A program may use at most 64 MiB of HBM per device.

v0:
```python
import functools
import math

import jax
import jax.numpy as jnp
from jax import lax
from jax.experimental import pallas as pl
from jax.experimental.pallas import tpu as pltpu
from jax.sharding import PartitionSpec as P

MESH = pl.DeviceIdType.MESH
F32, BF16 = jnp.float32, jnp.bfloat16

PLANES = (1, 7, 6, 3, 0, 5, 4, 2)
PAIRS = tuple(PLANES.index(z) for z in range(8))

NE = 32
B = 256
ROWS = B // NE
FACTOR = 1.0 / (math.sqrt(NE) * NE)

GREEN, POL, SCR, SIG = 0, 2, 4, 6
POL_NEXT, SCR_PREV, SIG_NEXT, OUT_PREV, BARE, SPREAD = 8, 9, 10, 11, 12, 13
KINDS = 14


def look_up(values, index):
    packed = sum(v << (3 * i) for i, v in enumerate(values))
    return lax.rem(lax.shift_right_logical(jnp.int32(packed), 3 * index), 8)


def rows_of(r):
    return pl.ds(pl.multiple_of(r * ROWS, ROWS), ROWS)


def split(values):
    high = values.astype(BF16)
    return high, (values - high.astype(F32)).astype(BF16)


def dot3(left, right):
    dot = functools.partial(jnp.dot, preferred_element_type=F32)
    return dot(left[0], right[0]) + dot(left[0], right[1]) + dot(left[1], right[0])


def times_root(real, imaginary, j, half, sign):
    if j == 0:
        return real, imaginary
    if 2 * j == half:
        return (-imaginary, real) if sign > 0 else (imaginary, -real)
    c = math.cos(math.pi * j / half)
    s = sign * math.sin(math.pi * j / half)
    return real * c - imaginary * s, imaginary * c + real * s


def forward(real, imaginary):
    real, imaginary = list(real), list(imaginary)
    half = NE // 2
    while half:
        for first in range(0, NE, 2 * half):
            for j in range(half):
                p, q = first + j, first + j + half
                dr, di = real[p] - real[q], imaginary[p] - imaginary[q]
                real[p], imaginary[p] = real[p] + real[q], imaginary[p] + imaginary[q]
                real[q], imaginary[q] = times_root(dr, di, j, half, -1)
        half //= 2
    return real, imaginary


def inverse(real, imaginary):
    real, imaginary = list(real), list(imaginary)
    half = 1
    while half < NE:
        for first in range(0, NE, 2 * half):
            for j in range(half):
                p, q = first + j, first + j + half
                br, bi = times_root(real[q], imaginary[q], j, half, 1)
                real[q], imaginary[q] = real[p] - br, imaginary[p] - bi
                real[p], imaginary[p] = real[p] + br, imaginary[p] + bi
        half *= 2
    return real, imaginary


def kernel(
    green, retarded_diag, retarded_upper, coulomb_diag, coulomb_upper, out,
    lg, ps, pp, wb, wr, ss, sb, c_send, c_prev, o_send, o_prev, vraw, rraw, ob,
    vh, vl, rh, rl, sh, sl, snd, rcv, loc,
):
    e, d = lax.axis_index("energy"), lax.axis_index("cell")
    zh, x, y = e // 16, (e // 4) % 4, e % 4
    core = d % 2
    z = zh * 4 + d // 2
    r = (x * 4 + y) * 2 + core
    k = look_up(PAIRS, z)
    target = look_up(PLANES, d)

    def at_plane(plane, slot):
        return ((plane // 4) * 16 + slot // 2, (plane % 4) * 2 + slot % 2)

    def slot_at(j):
        return (((x + j // 8) % 4) * 4 + (y + (j // 2) % 4) % 4) * 2 + (core + j % 2) % 2

    def energy_at(j):
        return ((zh + j % 2) % 2) * 16 + ((x + j // 8) % 4) * 4 + (y + (j // 2) % 4) % 4

    def remote(src, dst, kind, device):
        return pltpu.make_async_remote_copy(
            src, dst, snd.at[kind], rcv.at[kind], device_id=device, device_id_type=MESH
        )

    def wait_for(ref, sem):
        pltpu.make_async_copy(ref, ref, sem).wait()

    upper_plane = at_plane(look_up(PLANES, (k + 1) % 8), r)
    lower_plane = at_plane(look_up(PLANES, (k + 7) % 8), r)

    barrier = pltpu.get_barrier_semaphore()

    def greet(device):
        pl.semaphore_signal(barrier, inc=1, device_id=device, device_id_type=MESH)

    @pl.loop(0, NE)
    def _(j):
        greet(at_plane(target, slot_at(j)))
        greet((energy_at(j), k))

    @pl.loop(1, NE)
    def _(j):
        greet(at_plane(z, slot_at(j)))

    pl.when(k < 7)(lambda: greet(upper_plane))
    pl.when(k > 0)(lambda: greet(lower_plane))
    pl.when(d < 7)(lambda: greet((e, d + 1)))
    pl.when(d > 0)(lambda: greet((e, d - 1)))
    expected = 3 * NE - 1 + sum(jnp.where(t, 1, 0) for t in (k < 7, k > 0, d < 7, d > 0))
    pl.semaphore_wait(barrier, expected)

    bare = (x * 4 + y) * 2 + zh
    bare_device = at_plane(target, bare)
    remote(coulomb_diag.at[:, rows_of(bare), :], vraw.at[pl.ds(0, 2), rows_of(bare), :], BARE, bare_device).start()
    remote(coulomb_upper.at[:, rows_of(bare), :], vraw.at[pl.ds(2, 2), rows_of(bare), :], BARE, bare_device).start()

    for c in range(2):

        @pl.loop(0, NE)
        def _(j):
            slot = slot_at(j)
            remote(
                green.at[:, 0, c, rows_of(slot), :], lg.at[c, e], GREEN + c, at_plane(target, slot)
            ).start()

    load_diag = pltpu.make_async_copy(retarded_diag.at[:, 0], rraw.at[0], loc.at[0])
    load_upper = pltpu.make_async_copy(retarded_upper.at[:, 0], rraw.at[1], loc.at[1])
    load_diag.start()
    load_upper.start()

    wait_for(vraw.at[:, pl.ds(0, ROWS), :], rcv.at[BARE])

    @pl.loop(1, NE)
    def _(j):
        remote(
            vraw.at[:, rows_of(r), :], vraw.at[:, rows_of(r), :], SPREAD, at_plane(z, slot_at(j))
        ).start()

    load_diag.wait()
    load_upper.wait()

    @pl.loop(0, 8)
    def _(i):
        kind, plane, c = i // 4, (i // 2) % 2, i % 2
        block = rraw[kind, plane, c]
        at = kind * 4 + c * 2
        rh[at, plane], rl[at, plane] = split(block)
        rh[at + 1, plane], rl[at + 1, plane] = split(block.T)

    wait_for(vraw.at[:, pl.ds(0, B - ROWS), :], rcv.at[SPREAD])

    @pl.loop(0, 2)
    def _(c):
        block = vraw[c]
        vh[c], vl[c] = split((block + block.T) * 0.5)
        block = vraw[2 + c]
        vh[2 + 2 * c], vl[2 + 2 * c] = split(block)
        vh[3 + 2 * c], vl[3 + 2 * c] = split(block.T)

    @pl.loop(0, 2)
    def _(c):
        wait_for(lg.at[c], rcv.at[GREEN + c])

        @pl.loop(0, 2)
        def _(t):
            lanes = pl.ds(pl.multiple_of(t * 128, 128), 128)

            def load(plane):
                return [lg[c, n, plane, :, lanes] for n in range(NE)]

            l_re, l_im = forward(load(0), load(1))
            for n in range(NE):
                lg[c, n, 0, :, lanes] = l_re[n]
                lg[c, n, 1, :, lanes] = l_im[n]
            g_re, g_im = forward(load(2), load(3))
            l_re, l_im = load(0), load(1)
            re = [l_re[n] * g_re[n] + l_im[n] * g_im[n] for n in range(NE)]
            im = [l_im[n] * g_re[n] - l_re[n] * g_im[n] for n in range(NE)]
            re, im = inverse(re, im)
            for n in range(NE):
                ps[c, n, 0, :, lanes] = im[n] * -FACTOR
                ps[c, n, 1, :, lanes] = re[n] * FACTOR

        pltpu.make_async_copy(ps.at[c, r], pp.at[c, :, rows_of(r), :], rcv.at[POL + c]).start()

        @pl.loop(1, NE)
        def _(j):
            slot = slot_at(j)
            remote(
                ps.at[c, slot], pp.at[c, :, rows_of(r), :], POL + c, at_plane(z, slot)
            ).start()

    def screen(first, last, source, plane):
        inner = dot3((vh[first], vl[first]), split(pp[source, plane]))
        return dot3(split(inner), (vh[last], vl[last]))

    wait_for(pp.at[0], rcv.at[POL])
    pol_next = remote(pp.at[0], pp.at[2], POL_NEXT, lower_plane)
    pl.when(k > 0)(pol_next.start)

    @pl.loop(0, 2)
    def _(q):
        wb[0, q] = screen(0, 0, 0, q)
        wb[1, q] = screen(3, 2, 0, q)

    wait_for(pp.at[1], rcv.at[POL + 1])

    @pl.loop(0, 2)
    def _(q):
        c_send[q] = screen(5, 4, 1, q)

    scr_prev = remote(c_send, c_prev, SCR_PREV, upper_plane)
    pl.when(k < 7)(scr_prev.start)

    @pl.loop(0, 2)
    def _(q):
        wb[1, q] += screen(1, 1, 1, q)
        wb[0, q] += screen(2, 3, 1, q)

    def send_screened(c):
        pltpu.make_async_copy(wb.at[c, :, rows_of(r), :], wr.at[c, r], rcv.at[SCR + c]).start()

        @pl.loop(1, NE)
        def _(j):
            slot = slot_at(j)
            remote(
                wb.at[c, :, rows_of(slot), :], wr.at[c, r], SCR + c, at_plane(z, slot)
            ).start()

    @pl.when(k < 7)
    def _():
        wait_for(pp.at[2], rcv.at[POL_NEXT])

        @pl.loop(0, 2)
        def _(q):
            wb[1, q] += screen(4, 5, 2, q)

    send_screened(1)

    @pl.when(k > 0)
    def _():
        wait_for(c_prev, rcv.at[SCR_PREV])
        wb[0] += c_prev[...]

    send_screened(0)

    @pl.loop(0, 2)
    def _(i):
        c = 1 - i
        wait_for(wr.at[c], rcv.at[SCR + c])

        @pl.loop(0, 2)
        def _(t):
            lanes = pl.ds(pl.multiple_of(t * 128, 128), 128)
            w_re, w_im = forward(
                [wr[c, n, 0, :, lanes] for n in range(NE)],
                [wr[c, n, 1, :, lanes] for n in range(NE)],
            )
            l_re = [lg[c, n, 0, :, lanes] for n in range(NE)]
            l_im = [lg[c, n, 1, :, lanes] for n in range(NE)]
            re = [l_re[n] * w_re[n] - l_im[n] * w_im[n] for n in range(NE)]
            im = [l_re[n] * w_im[n] + l_im[n] * w_re[n] for n in range(NE)]
            re, im = inverse(re, im)
            for n in range(NE):
                ss[c, n, 0, :, lanes] = im[n] * -FACTOR
                ss[c, n, 1, :, lanes] = re[n] * FACTOR

        @pl.loop(0, NE)
        def _(j):
            n = energy_at(j)
            remote(ss.at[c, n], sb.at[c, :, rows_of(r), :], SIG + c, (n, k)).start()

    def split_sigma(s):
        @pl.loop(0, 2)
        def _(q):
            sh[q], sl[q] = split(sb[s, q])

    def dress(left, right, half):
        rows = pl.ds(pl.multiple_of(half * 128, 128), 128)
        l_re = (rh[left, 0, rows], rl[left, 0, rows])
        l_im = (rh[left, 1, rows], rl[left, 1, rows])
        s_re, s_im = (sh[0], sl[0]), (sh[1], sl[1])
        t_re = split(dot3(l_re, s_re) - dot3(l_im, s_im))
        t_im = split(dot3(l_re, s_im) + dot3(l_im, s_re))
        b_re = (rh[right, 0], rl[right, 0])
        b_im = (rh[right, 1], rl[right, 1])
        return rows, dot3(t_re, b_re) + dot3(t_im, b_im), dot3(t_im, b_re) - dot3(t_re, b_im)

    wait_for(sb.at[1], rcv.at[SIG + 1])
    split_sigma(1)

    @pl.loop(0, 2)
    def _(half):
        rows, re, im = dress(7, 6, half)
        o_send[0, rows] = re
        o_send[1, rows] = im

    out_prev = remote(o_send, o_prev, OUT_PREV, (e, (d + 1) % 8))
    pl.when(d < 7)(out_prev.start)

    @pl.loop(0, 4)
    def _(i):
        c, half = 1 - i // 2, i % 2
        rows, re, im = dress(2 + 2 * (i // 2), 3 + 2 * (i // 2), half)
        ob[0, c, rows] = re
        ob[1, c, rows] = im

    wait_for(sb.at[0], rcv.at[SIG])
    sig_next = remote(sb.at[0], sb.at[2], SIG_NEXT, (e, (d + 7) % 8))
    pl.when(d > 0)(sig_next.start)
    split_sigma(0)

    @pl.loop(0, 4)
    def _(i):
        c, half = i // 2, i % 2
        rows, re, im = dress(5 * c, 1 + 3 * c, half)
        ob[0, c, rows] += re
        ob[1, c, rows] += im

    @pl.when(d > 0)
    def _():
        wait_for(o_prev, rcv.at[OUT_PREV])
        ob[:, 0] += o_prev[...]

    store_a = pltpu.make_async_copy(ob.at[:, 0], out.at[:, 0, 0], loc.at[0])
    store_a.start()

    @pl.when(d < 7)
    def _():
        wait_for(sb.at[2], rcv.at[SIG_NEXT])
        split_sigma(2)

        @pl.loop(0, 2)
        def _(half):
            rows, re, im = dress(6, 7, half)
            ob[0, 1, rows] += re
            ob[1, 1, rows] += im

    store_b = pltpu.make_async_copy(ob.at[:, 1], out.at[:, 0, 1], loc.at[1])
    store_b.start()

    wait_for(vraw.at[:, pl.ds(0, ROWS), :], snd.at[BARE])
    wait_for(vraw.at[:, pl.ds(0, B - ROWS), :], snd.at[SPREAD])
    for c in range(2):
        wait_for(lg.at[c], snd.at[GREEN + c])
        wait_for(ps.at[c, pl.ds(0, NE - 1)], snd.at[POL + c])
        wait_for(wr.at[c, pl.ds(0, NE - 1)], snd.at[SCR + c])
        wait_for(ss.at[c], snd.at[SIG + c])
    pl.when(k > 0)(pol_next.wait_send)
    pl.when(k < 7)(scr_prev.wait_send)
    pl.when(d > 0)(sig_next.wait_send)
    pl.when(d < 7)(out_prev.wait_send)
    store_a.wait()
    store_b.wait()


def per_device(*arrays):
    block = (2, B, B)
    slices = (2, NE, 2, ROWS, B)
    return pl.pallas_call(
        kernel,
        out_shape=jax.ShapeDtypeStruct((2, 1, 2, B, B), F32),
        in_specs=[pl.BlockSpec(memory_space=pl.ANY)] * 5,
        out_specs=pl.BlockSpec(memory_space=pl.ANY),
        scratch_shapes=[
            pltpu.VMEM((2, NE, 4, ROWS, B), F32),
            pltpu.VMEM(slices, F32),
            pltpu.VMEM((3,) + block, F32),
            pltpu.VMEM((2,) + block, F32),
            pltpu.VMEM(slices, F32),
            pltpu.VMEM(slices, F32),
            pltpu.VMEM((3,) + block, F32),
            pltpu.VMEM(block, F32),
            pltpu.VMEM(block, F32),
            pltpu.VMEM(block, F32),
            pltpu.VMEM(block, F32),
            pltpu.VMEM((4, B, B), F32),
            pltpu.VMEM((2, 2) + block, F32),
            pltpu.VMEM((2,) + block, F32),
            pltpu.VMEM((6, B, B), BF16),
            pltpu.VMEM((6, B, B), BF16),
            pltpu.VMEM((8,) + block, BF16),
            pltpu.VMEM((8,) + block, BF16),
            pltpu.VMEM(block, BF16),
            pltpu.VMEM(block, BF16),
            pltpu.SemaphoreType.DMA((KINDS,)),
            pltpu.SemaphoreType.DMA((KINDS,)),
            pltpu.SemaphoreType.DMA((2,)),
        ],
        compiler_params=pltpu.CompilerParams(
            collective_id=0, has_side_effects=True, vmem_limit_bytes=56 << 20
        ),
        name="self_energy",
    )(*arrays)


def solution(mesh):
    in_specs = (
        P(None, "energy", "cell", None, None),
        P(None, "energy", "cell", None, None),
        P(None, "energy", "cell", None, None),
        P("cell", None, None),
        P("cell", None, None),
    )
    out_specs = P(None, "energy", "cell", None, None)
    return jax.shard_map(
        per_device, mesh=mesh, in_specs=in_specs, out_specs=out_specs, check_vma=False
    )
```

profile of v0, /device:TPU:1, one launch (start us, length us, event | category | flops | bytes accessed | tf_op | source)
XLA Modules:
  0.0 143.6 jit_solution(758425736471257081)
XLA Ops:
  0.0 141.3 %self_energy.1 = f32[2,1,2,256,256]{4,3,2,1,0:T(8,128)} custom-call(f32[4,1,2,256,256]{4,3,2,1,0:T(8,128)} %green.1, f32[2,1,2,256,256]{4,3,2,1,0:T(8,128)} %retarded_diag.1, f32[2,1,2,256,256]{4,3,2,1,0:T(8,128)} %retarded_upper.1, f32[2,256,256]{2,1,0:T(8,128)} %coulomb_diag.1, f32[2,256,256]{2,1,0:T(8,128)} %coulomb_upper.1), custom_call_target="tpu_custom_call" | custom-call | tf_op jit(solution)/shard_map/self_energy/pallas_call | solution.py:386
  141.3 2.3 %copy.7 = f32[2,1,2,256,256]{4,3,2,1,0:T(8,128)} copy(f32[2,1,2,256,256]{4,3,2,1,0:T(8,128)} %self_energy.1) | data formatting | bytes 2097152
where the time goes:
time: 144 us
  Pallas kernels  141 us (98%)
  local copies, waits for them, and re-layouts  2.29 us (2%)
    pallas_call x1, Pallas kernels, per_device(): pl.pallas_call(kernel, out_shape=jax.ShapeDtypeStruct((2, 1, 2, B, B), F3...  141 us

commit v1 on v0

--- a/solution.py
+++ b/solution.py
@@ -11,7 +11,7 @@
 MESH = pl.DeviceIdType.MESH
 F32, BF16 = jnp.float32, jnp.bfloat16
 
-PLANES = (1, 7, 6, 3, 0, 5, 4, 2)
+PLANES = (2, 7, 6, 4, 3, 1, 0, 5)
 PAIRS = tuple(PLANES.index(z) for z in range(8))
 
 NE = 32
@@ -94,14 +94,20 @@
     k = look_up(PAIRS, z)
     target = look_up(PLANES, d)
 
+    def cell_at(step):
+        return lax.rem(jnp.where(k < 4, 1, 0) + step, 2)
+
+    def own_cell_at(step):
+        return lax.rem(jnp.where(d < 4, 1, 0) + step, 2)
+
     def at_plane(plane, slot):
         return ((plane // 4) * 16 + slot // 2, (plane % 4) * 2 + slot % 2)
 
     def slot_at(j):
-        return (((x + j // 8) % 4) * 4 + (y + (j // 2) % 4) % 4) * 2 + (core + j % 2) % 2
+        return (((x + j // 2) % 4) * 4 + (y + j // 2 + j // 8) % 4) * 2 + (core + j) % 2
 
     def energy_at(j):
-        return ((zh + j % 2) % 2) * 16 + ((x + j // 8) % 4) * 4 + (y + (j // 2) % 4) % 4
+        return ((zh + j) % 2) * 16 + ((x + j // 2) % 4) * 4 + (y + j // 2 + j // 8) % 4
 
     def remote(src, dst, kind, device):
         return pltpu.make_async_remote_copy(
@@ -140,13 +146,14 @@
     remote(coulomb_diag.at[:, rows_of(bare), :], vraw.at[pl.ds(0, 2), rows_of(bare), :], BARE, bare_device).start()
     remote(coulomb_upper.at[:, rows_of(bare), :], vraw.at[pl.ds(2, 2), rows_of(bare), :], BARE, bare_device).start()
 
-    for c in range(2):
+    for step in range(2):
+        c = own_cell_at(step)
 
         @pl.loop(0, NE)
         def _(j):
             slot = slot_at(j)
             remote(
-                green.at[:, 0, c, rows_of(slot), :], lg.at[c, e], GREEN + c, at_plane(target, slot)
+                green.at[:, 0, c, rows_of(slot), :], lg.at[c, e], GREEN + step, at_plane(target, slot)
             ).start()
 
     load_diag = pltpu.make_async_copy(retarded_diag.at[:, 0], rraw.at[0], loc.at[0])
@@ -173,19 +180,12 @@
         rh[at, plane], rl[at, plane] = split(block)
         rh[at + 1, plane], rl[at + 1, plane] = split(block.T)
 
-    wait_for(vraw.at[:, pl.ds(0, B - ROWS), :], rcv.at[SPREAD])
-
-    @pl.loop(0, 2)
-    def _(c):
-        block = vraw[c]
-        vh[c], vl[c] = split((block + block.T) * 0.5)
-        block = vraw[2 + c]
-        vh[2 + 2 * c], vl[2 + 2 * c] = split(block)
-        vh[3 + 2 * c], vl[3 + 2 * c] = split(block.T)
-
-    @pl.loop(0, 2)
-    def _(c):
-        wait_for(lg.at[c], rcv.at[GREEN + c])
+    wb[...] = jnp.zeros_like(wb)
+    ob[...] = jnp.zeros_like(ob)
+
+    def polarize(step):
+        c = cell_at(step)
+        wait_for(lg.at[c], rcv.at[GREEN + step])
 
         @pl.loop(0, 2)
         def _(t):
@@ -207,73 +207,91 @@
                 ps[c, n, 0, :, lanes] = im[n] * -FACTOR
                 ps[c, n, 1, :, lanes] = re[n] * FACTOR
 
-        pltpu.make_async_copy(ps.at[c, r], pp.at[c, :, rows_of(r), :], rcv.at[POL + c]).start()
+            pltpu.make_async_copy(
+                ps.at[c, r, :, :, lanes], pp.at[c, :, rows_of(r), lanes], rcv.at[POL + step]
+            ).start()
+
+            @pl.loop(1, NE)
+            def _(j):
+                slot = slot_at(j)
+                remote(
+                    ps.at[c, slot, :, :, lanes],
+                    pp.at[c, :, rows_of(r), lanes],
+                    POL + step,
+                    at_plane(z, slot),
+                ).start()
+
+    def bare_blocks():
+        wait_for(vraw.at[:, pl.ds(0, B - ROWS), :], rcv.at[SPREAD])
+
+        @pl.loop(0, 2)
+        def _(c):
+            block = vraw[c]
+            vh[c], vl[c] = split((block + block.T) * 0.5)
+            block = vraw[2 + c]
+            vh[2 + 2 * c], vl[2 + 2 * c] = split(block)
+            vh[3 + 2 * c], vl[3 + 2 * c] = split(block.T)
+
+    def screen(first, last, source, plane):
+        inner = dot3((vh[first], vl[first]), split(pp[source, plane]))
+        return dot3(split(inner), (vh[last], vl[last]))
+
+    pol_next = remote(pp.at[0], pp.at[2], POL_NEXT, lower_plane)
+    scr_prev = remote(c_send, c_prev, SCR_PREV, upper_plane)
+
+    def spread_polarization(step):
+        c = cell_at(step)
+        wait_for(pp.at[c], rcv.at[POL + step])
+        pl.when((c == 0) & (k > 0))(pol_next.start)
+
+        @pl.when((c == 1) & (k < 7))
+        def _():
+            @pl.loop(0, 2)
+            def _(q):
+                c_send[q] = screen(5, 4, 1, q)
+                remote(c_send.at[q], c_prev.at[q], SCR_PREV, upper_plane).start()
+
+        @pl.loop(0, 2)
+        def _(q):
+            wb[c, q] += screen(c, c, c, q)
+            wb[1 - c, q] += screen(3 - c, 2 + c, c, q)
+
+    @pl.loop(0, 2)
+    def _(step):
+        polarize(step)
+        pl.when(step == 0)(bare_blocks)
+        spread_polarization(step)
+
+    @pl.loop(0, 2)
+    def _(step):
+        c = cell_at(step + 1)
+
+        @pl.when((c == 1) & (k < 7))
+        def _():
+            wait_for(pp.at[2], rcv.at[POL_NEXT])
+
+            @pl.loop(0, 2)
+            def _(q):
+                wb[1, q] += screen(4, 5, 2, q)
+
+        @pl.when((c == 0) & (k > 0))
+        def _():
+            wait_for(c_prev, rcv.at[SCR_PREV])
+            wb[0] += c_prev[...]
+
+        pltpu.make_async_copy(wb.at[c, :, rows_of(r), :], wr.at[c, r], rcv.at[SCR + step]).start()
 
         @pl.loop(1, NE)
         def _(j):
             slot = slot_at(j)
             remote(
-                ps.at[c, slot], pp.at[c, :, rows_of(r), :], POL + c, at_plane(z, slot)
+                wb.at[c, :, rows_of(slot), :], wr.at[c, r], SCR + step, at_plane(z, slot)
             ).start()
 
-    def screen(first, last, source, plane):
-        inner = dot3((vh[first], vl[first]), split(pp[source, plane]))
-        return dot3(split(inner), (vh[last], vl[last]))
-
-    wait_for(pp.at[0], rcv.at[POL])
-    pol_next = remote(pp.at[0], pp.at[2], POL_NEXT, lower_plane)
-    pl.when(k > 0)(pol_next.start)
-
     @pl.loop(0, 2)
-    def _(q):
-        wb[0, q] = screen(0, 0, 0, q)
-        wb[1, q] = screen(3, 2, 0, q)
-
-    wait_for(pp.at[1], rcv.at[POL + 1])
-
-    @pl.loop(0, 2)
-    def _(q):
-        c_send[q] = screen(5, 4, 1, q)
-
-    scr_prev = remote(c_send, c_prev, SCR_PREV, upper_plane)
-    pl.when(k < 7)(scr_prev.start)
-
-    @pl.loop(0, 2)
-    def _(q):
-        wb[1, q] += screen(1, 1, 1, q)
-        wb[0, q] += screen(2, 3, 1, q)
-
-    def send_screened(c):
-        pltpu.make_async_copy(wb.at[c, :, rows_of(r), :], wr.at[c, r], rcv.at[SCR + c]).start()
-
-        @pl.loop(1, NE)
-        def _(j):
-            slot = slot_at(j)
-            remote(
-                wb.at[c, :, rows_of(slot), :], wr.at[c, r], SCR + c, at_plane(z, slot)
-            ).start()
-
-    @pl.when(k < 7)
-    def _():
-        wait_for(pp.at[2], rcv.at[POL_NEXT])
-
-        @pl.loop(0, 2)
-        def _(q):
-            wb[1, q] += screen(4, 5, 2, q)
-
-    send_screened(1)
-
-    @pl.when(k > 0)
-    def _():
-        wait_for(c_prev, rcv.at[SCR_PREV])
-        wb[0] += c_prev[...]
-
-    send_screened(0)
-
-    @pl.loop(0, 2)
-    def _(i):
-        c = 1 - i
-        wait_for(wr.at[c], rcv.at[SCR + c])
+    def _(step):
+        c = cell_at(step + 1)
+        wait_for(wr.at[c], rcv.at[SCR + step])
 
         @pl.loop(0, 2)
         def _(t):
@@ -294,7 +312,7 @@
         @pl.loop(0, NE)
         def _(j):
             n = energy_at(j)
-            remote(ss.at[c, n], sb.at[c, :, rows_of(r), :], SIG + c, (n, k)).start()
+            remote(ss.at[c, n], sb.at[c, :, rows_of(r), :], SIG + step, (n, k)).start()
 
     def split_sigma(s):
         @pl.loop(0, 2)
@@ -312,58 +330,54 @@
         b_im = (rh[right, 1], rl[right, 1])
         return rows, dot3(t_re, b_re) + dot3(t_im, b_im), dot3(t_im, b_re) - dot3(t_re, b_im)
 
-    wait_for(sb.at[1], rcv.at[SIG + 1])
-    split_sigma(1)
+    sig_next = remote(sb.at[0], sb.at[2], SIG_NEXT, (e, (d + 7) % 8))
+    out_prev = remote(o_send, o_prev, OUT_PREV, (e, (d + 1) % 8))
 
     @pl.loop(0, 2)
-    def _(half):
-        rows, re, im = dress(7, 6, half)
-        o_send[0, rows] = re
-        o_send[1, rows] = im
-
-    out_prev = remote(o_send, o_prev, OUT_PREV, (e, (d + 1) % 8))
-    pl.when(d < 7)(out_prev.start)
-
-    @pl.loop(0, 4)
-    def _(i):
-        c, half = 1 - i // 2, i % 2
-        rows, re, im = dress(2 + 2 * (i // 2), 3 + 2 * (i // 2), half)
-        ob[0, c, rows] = re
-        ob[1, c, rows] = im
-
-    wait_for(sb.at[0], rcv.at[SIG])
-    sig_next = remote(sb.at[0], sb.at[2], SIG_NEXT, (e, (d + 7) % 8))
-    pl.when(d > 0)(sig_next.start)
-    split_sigma(0)
-
-    @pl.loop(0, 4)
-    def _(i):
-        c, half = i // 2, i % 2
-        rows, re, im = dress(5 * c, 1 + 3 * c, half)
-        ob[0, c, rows] += re
-        ob[1, c, rows] += im
-
-    @pl.when(d > 0)
-    def _():
-        wait_for(o_prev, rcv.at[OUT_PREV])
-        ob[:, 0] += o_prev[...]
-
-    store_a = pltpu.make_async_copy(ob.at[:, 0], out.at[:, 0, 0], loc.at[0])
-    store_a.start()
-
-    @pl.when(d < 7)
-    def _():
-        wait_for(sb.at[2], rcv.at[SIG_NEXT])
-        split_sigma(2)
-
-        @pl.loop(0, 2)
-        def _(half):
-            rows, re, im = dress(6, 7, half)
-            ob[0, 1, rows] += re
-            ob[1, 1, rows] += im
-
-    store_b = pltpu.make_async_copy(ob.at[:, 1], out.at[:, 0, 1], loc.at[1])
-    store_b.start()
+    def _(step):
+        c = own_cell_at(step + 1)
+        wait_for(sb.at[c], rcv.at[SIG + step])
+        pl.when((c == 0) & (d > 0))(sig_next.start)
+        split_sigma(c)
+
+        @pl.when((c == 1) & (d < 7))
+        def _():
+            @pl.loop(0, 2)
+            def _(half):
+                rows, re, im = dress(7, 6, half)
+                o_send[0, rows] = re
+                o_send[1, rows] = im
+                remote(o_send.at[:, rows], o_prev.at[:, rows], OUT_PREV, (e, (d + 1) % 8)).start()
+
+        @pl.loop(0, 4)
+        def _(i):
+            to, half = (c + i // 2) % 2, i % 2
+            other = i // 2
+            rows, re, im = dress(2 * c + other * (5 - 3 * c), 2 * c + 1 + other * (3 - c), half)
+            ob[0, to, rows] += re
+            ob[1, to, rows] += im
+
+    @pl.loop(0, 2)
+    def _(step):
+        c = own_cell_at(step)
+
+        @pl.when((c == 0) & (d > 0))
+        def _():
+            wait_for(o_prev, rcv.at[OUT_PREV])
+            ob[:, 0] += o_prev[...]
+
+        @pl.when((c == 1) & (d < 7))
+        def _():
+            wait_for(sb.at[2], rcv.at[SIG_NEXT])
+            split_sigma(2)
+
+            @pl.loop(0, 2)
+            def _(half):
+                rows, re, im = dress(6, 7, half)
+                ob[0, 1, rows] += re
+                ob[1, 1, rows] += im
+
+        pltpu.make_async_copy(ob.at[:, c], out.at[:, 0, c], loc.at[step]).start()
 
     wait_for(vraw.at[:, pl.ds(0, ROWS), :], snd.at[BARE])
     wait_for(vraw.at[:, pl.ds(0, B - ROWS), :], snd.at[SPREAD])
@@ -376,8 +390,8 @@
     pl.when(k < 7)(scr_prev.wait_send)
     pl.when(d > 0)(sig_next.wait_send)
     pl.when(d < 7)(out_prev.wait_send)
-    store_a.wait()
-    store_b.wait()
+    for step in range(2):
+        wait_for(ob.at[:, step], loc.at[step])
 
 
 def per_device(*arrays):

time: 144 us -> 132 us (0.917); the launches traced: 144 us -> 129 us
  Pallas kernels: 141 us -> 127 us
    pallas_call x1, Pallas kernels: 141 us -> 127 us  [per_device(): pl.pallas_call(kernel, out_shape=jax.ShapeDtypeStruct((2, 1, 2, B, B), F3...]
where the time goes in v1:
time: 132 us; the launch traced here: 129 us
  Pallas kernels  127 us (96%)
  local copies, waits for them, and re-layouts  2.29 us (2%)
    pallas_call x1, Pallas kernels, per_device(): pl.pallas_call(kernel, out_shape=jax.ShapeDtypeStruct((2, 1, 2, B, B), F3...  127 us

profile of v1, /device:TPU:1, one launch (start us, length us, event | category | flops | bytes accessed | tf_op | source)
XLA Modules:
  0.0 129.4 jit_solution(10447691909347566890)
XLA Ops:
  0.0 127.1 %self_energy.1 = f32[2,1,2,256,256]{4,3,2,1,0:T(8,128)} custom-call(f32[4,1,2,256,256]{4,3,2,1,0:T(8,128)} %green.1, f32[2,1,2,256,256]{4,3,2,1,0:T(8,128)} %retarded_diag.1, f32[2,1,2,256,256]{4,3,2,1,0:T(8,128)} %retarded_upper.1, f32[2,256,256]{2,1,0:T(8,128)} %coulomb_diag.1, f32[2,256,256]{2,1,0:T(8,128)} %coulomb_upper.1), custom_call_target="tpu_custom_call" | custom-call | tf_op jit(solution)/shard_map/self_energy/pallas_call | solution.py:400
  127.1 2.3 %copy.7 = f32[2,1,2,256,256]{4,3,2,1,0:T(8,128)} copy(f32[2,1,2,256,256]{4,3,2,1,0:T(8,128)} %self_energy.1) | data formatting | bytes 2097152

commit v2 on v1

--- a/solution.py
+++ b/solution.py
@@ -103,10 +103,14 @@
     def at_plane(plane, slot):
         return ((plane // 4) * 16 + slot // 2, (plane % 4) * 2 + slot % 2)
 
+    turn = 16 * core + 8 * (z % 2)
+
     def slot_at(j):
+        j = j % NE
         return (((x + j // 2) % 4) * 4 + (y + j // 2 + j // 8) % 4) * 2 + (core + j) % 2
 
     def energy_at(j):
+        j = j % NE
         return ((zh + j) % 2) * 16 + ((x + j // 2) % 4) * 4 + (y + j // 2 + j // 8) % 4
 
     def remote(src, dst, kind, device):
@@ -151,7 +155,7 @@
 
         @pl.loop(0, NE)
         def _(j):
-            slot = slot_at(j)
+            slot = slot_at(j + turn)
             remote(
                 green.at[:, 0, c, rows_of(slot), :], lg.at[c, e], GREEN + step, at_plane(target, slot)
             ).start()
@@ -166,7 +170,7 @@
     @pl.loop(1, NE)
     def _(j):
         remote(
-            vraw.at[:, rows_of(r), :], vraw.at[:, rows_of(r), :], SPREAD, at_plane(z, slot_at(j))
+            vraw.at[:, rows_of(r), :], vraw.at[:, rows_of(r), :], SPREAD, at_plane(z, slot_at(1 + (j - 1 + turn) % (NE - 1)))
         ).start()
 
     load_diag.wait()
@@ -213,7 +217,7 @@
 
             @pl.loop(1, NE)
             def _(j):
-                slot = slot_at(j)
+                slot = slot_at(1 + (j - 1 + turn) % (NE - 1))
                 remote(
                     ps.at[c, slot, :, :, lanes],
                     pp.at[c, :, rows_of(r), lanes],
@@ -283,7 +287,7 @@
 
         @pl.loop(1, NE)
         def _(j):
-            slot = slot_at(j)
+            slot = slot_at(1 + (j - 1 + turn) % (NE - 1))
             remote(
                 wb.at[c, :, rows_of(slot), :], wr.at[c, r], SCR + step, at_plane(z, slot)
             ).start()
@@ -311,7 +315,7 @@
 
         @pl.loop(0, NE)
         def _(j):
-            n = energy_at(j)
+            n = energy_at(j + turn)
             remote(ss.at[c, n], sb.at[c, :, rows_of(r), :], SIG + step, (n, k)).start()
 
     def split_sigma(s):

time: 132 us -> 129 us (0.977); the launches traced: 129 us -> 128 us
    pallas_call x1, Pallas kernels: 127 us -> 126 us  [per_device(): pl.pallas_call(kernel, out_shape=jax.ShapeDtypeStruct((2, 1, 2, B, B), F3...]
where the time goes in v2:
time: 129 us; the launch traced here: 128 us
  Pallas kernels  126 us (98%)
  local copies, waits for them, and re-layouts  2.29 us (2%)
    pallas_call x1, Pallas kernels, per_device(): pl.pallas_call(kernel, out_shape=jax.ShapeDtypeStruct((2, 1, 2, B, B), F3...  126 us

profile of v2, /device:TPU:1, one launch (start us, length us, event | category | flops | bytes accessed | tf_op | source)
XLA Modules:
  0.0 128.0 jit_solution(17570938641384736350)
XLA Ops:
  0.0 125.7 %self_energy.1 = f32[2,1,2,256,256]{4,3,2,1,0:T(8,128)} custom-call(f32[4,1,2,256,256]{4,3,2,1,0:T(8,128)} %green.1, f32[2,1,2,256,256]{4,3,2,1,0:T(8,128)} %retarded_diag.1, f32[2,1,2,256,256]{4,3,2,1,0:T(8,128)} %retarded_upper.1, f32[2,256,256]{2,1,0:T(8,128)} %coulomb_diag.1, f32[2,256,256]{2,1,0:T(8,128)} %coulomb_upper.1), custom_call_target="tpu_custom_call" | custom-call | tf_op jit(solution)/shard_map/self_energy/pallas_call | solution.py:404
  125.7 2.3 %copy.7 = f32[2,1,2,256,256]{4,3,2,1,0:T(8,128)} copy(f32[2,1,2,256,256]{4,3,2,1,0:T(8,128)} %self_energy.1) | data formatting | bytes 2097152

commit v3 on v2

--- a/solution.py
+++ b/solution.py
@@ -313,10 +313,12 @@
                 ss[c, n, 0, :, lanes] = im[n] * -FACTOR
                 ss[c, n, 1, :, lanes] = re[n] * FACTOR
 
-        @pl.loop(0, NE)
-        def _(j):
-            n = energy_at(j + turn)
-            remote(ss.at[c, n], sb.at[c, :, rows_of(r), :], SIG + step, (n, k)).start()
+            @pl.loop(0, NE)
+            def _(j):
+                n = energy_at(j + turn)
+                remote(
+                    ss.at[c, n, :, :, lanes], sb.at[c, :, rows_of(r), lanes], SIG + step, (n, k)
+                ).start()
 
     def split_sigma(s):
         @pl.loop(0, 2)

time: 129 us -> 129 us (level)
  no operation moved by 1% of the time
where the time goes in v3:
time: 129 us; the launch traced here: 128 us
  Pallas kernels  125 us (97%)
  local copies, waits for them, and re-layouts  2.29 us (2%)
    pallas_call x1, Pallas kernels, per_device(): pl.pallas_call(kernel, out_shape=jax.ShapeDtypeStruct((2, 1, 2, B, B), F3...  125 us

profile of v3, /device:TPU:1, one launch (start us, length us, event | category | flops | bytes accessed | tf_op | source)
XLA Modules:
  0.0 127.8 jit_solution(17431173687502058317)
XLA Ops:
  0.0 125.5 %self_energy.1 = f32[2,1,2,256,256]{4,3,2,1,0:T(8,128)} custom-call(f32[4,1,2,256,256]{4,3,2,1,0:T(8,128)} %green.1, f32[2,1,2,256,256]{4,3,2,1,0:T(8,128)} %retarded_diag.1, f32[2,1,2,256,256]{4,3,2,1,0:T(8,128)} %retarded_upper.1, f32[2,256,256]{2,1,0:T(8,128)} %coulomb_diag.1, f32[2,256,256]{2,1,0:T(8,128)} %coulomb_upper.1), custom_call_target="tpu_custom_call" | custom-call | tf_op jit(solution)/shard_map/self_energy/pallas_call | solution.py:406
  125.5 2.3 %copy.7 = f32[2,1,2,256,256]{4,3,2,1,0:T(8,128)} copy(f32[2,1,2,256,256]{4,3,2,1,0:T(8,128)} %self_energy.1) | data formatting | bytes 2097152
